TPU v7x, 128 devices: a whole 4x4x4 slice. The times are simulated.
128 devices in a mesh: ctx: 4 (over z_lo, core), tp: 16 (over y, x), dp: 2 (over z_hi).
Axes of the slice: x: 4, y: 4, z: 4 (z_hi: 2, z_lo: 2; z = z_hi * 2 + z_lo), core: 2. Of those that a mesh axis runs over, the one named last changes fastest.
Arguments:
- hidden_in: bfloat16 [8192, 8192], P(('dp', 'ctx', 'tp')), parts along dimension 0
- norm_gain: float32 [8192], replicated
- q_weight: bfloat16 [8192, 8192], P(None, 'tp')
- kv_weight: bfloat16 [8192, 2048], P(None, 'tp')
- out_weight: bfloat16 [8192, 8192], P('tp'), may hold values from -0.25 to 0.25
- doc_lengths: int32 [16], P('dp'), parts along dimension 0, may hold values from 1 to 2048, 4096 in all
Outputs:
- attn_out: bfloat16 [8192, 8192], P(('dp', 'ctx', 'tp')), parts along dimension 0
There are 2 independent parts, one for each index of `dp`. A program takes and returns all parts, laid end to end along the dimension named above; an argument that names none is the same for every part. Nothing has to cross between parts.
Inputs may be any that keep to these rules, and one draw needn't show every extreme that they name: `doc_lengths`: the lengths of a row sum to 4096; the longest document has exactly 2048 tokens.
All inputs are finite; a program needn't handle non-finite values.
Results may differ from a plain program's by a relative error of at most 0.015.
The roundings to bfloat16 on the way count: a program that leaves them out, or rounds other values in their place, can miss the bound.
Values may be sent and summed in bfloat16 or wider, within the bound.
No kernel may reach another device: no remote copies, remote signals or barrier semaphores. Data moves between devices by JAX's collectives and lax.ppermute only.
A program may use at most 128 MiB of HBM per device.

v0:
```python
import math

import jax
import jax.numpy as jnp
from jax import lax
from jax.sharding import PartitionSpec as P

QH = 64
KVH = 8
HD = 128


def from_everyone(shard, axis):
    length = lax.axis_size(axis)
    return lax.all_to_all(
        jnp.broadcast_to(shard[None], (length, *shard.shape)), axis, 0, 0, tiled=True
    )


def laid_out(blocks, dim):
    blocks = jnp.moveaxis(blocks, 0, dim)
    shape = blocks.shape
    return blocks.reshape(*shape[:dim], shape[dim] * shape[dim + 1], *shape[dim + 2 :])


def gathered_copies(shard, axis, dim):
    blocks = from_everyone(shard, axis)
    return laid_out(blocks, dim)


def doc_index(positions, ends):
    return jnp.sum((positions[:, None] >= ends[None, :]).astype(jnp.int32), axis=1)


def doc_start(positions, lengths, ends):
    return jnp.sum(jnp.where(positions[:, None] >= ends[None, :], lengths[None, :], 0), axis=1)


def rope_freqs(half):
    base = jnp.power(jnp.float32(500000.0), -(jnp.arange(half, dtype=jnp.float32) * 2.0) / HD)
    wavelen = 2.0 * math.pi / base
    smooth = (8192.0 / wavelen - 1.0) / 3.0
    middle = (1.0 - smooth) * base / 8.0 + smooth * base
    return jnp.where(wavelen < 2048.0, base, jnp.where(wavelen > 8192.0, base / 8.0, middle))


def rotate(values, within):
    rows = values.shape[0]
    blocks = values.reshape(rows, values.shape[1] // HD, HD)
    half = HD // 2
    freqs = rope_freqs(half)
    angles = within.astype(jnp.float32)[:, None] * freqs[None, :]
    cosine = jnp.cos(angles)[:, None, :]
    sine = jnp.sin(angles)[:, None, :]
    first = blocks[:, :, :half]
    second = blocks[:, :, half:]
    turned = jnp.concatenate(
        [first * cosine - second * sine, second * cosine + first * sine], axis=2
    )
    return turned.reshape(rows, values.shape[1])


def local(hidden_in, norm_gain, q_weight, kv_weight, out_weight, doc_lengths):
    tok_rows = hidden_in.shape[0]
    n_tp = lax.axis_size("tp")
    n_ctx = lax.axis_size("ctx")
    ctx_rows = tok_rows * n_tp
    block_rows = ctx_rows // n_ctx
    q_cols = q_weight.shape[1]
    heads_here = q_cols // HD
    group = QH // KVH
    kv_here = max(1, heads_here // group)
    sub_heads = heads_here // kv_here
    kv_cols = kv_weight.shape[1]
    tp_index = lax.axis_index("tp")
    ctx_index = lax.axis_index("ctx")
    scale = HD ** (-0.5)
    x = hidden_in.astype(jnp.float32)
    normed = (
        x * lax.rsqrt(jnp.mean(x * x, axis=1, keepdims=True) + 1e-05) * norm_gain[None, :]
    ).astype(jnp.bfloat16)
    ends = jnp.cumsum(doc_lengths)
    is_key = tp_index * kv_cols < KVH * HD
    piece = lax.all_gather(normed, "tp", axis=0, tiled=True)
    count = piece.shape[0]
    positions = ctx_index * ctx_rows + jnp.arange(count, dtype=jnp.int32)
    within = positions - doc_start(positions, doc_lengths, ends)
    q_raw = jnp.dot(piece, q_weight, preferred_element_type=jnp.float32)
    kv_raw = jnp.dot(piece, kv_weight, preferred_element_type=jnp.float32)
    q_done = rotate(q_raw, within).astype(jnp.bfloat16)
    kv_done = jnp.where(is_key, rotate(kv_raw, within), kv_raw).astype(jnp.bfloat16)
    projected = jnp.concatenate([q_done, kv_done], axis=1)
    queries = projected[:, :q_cols]
    kv_part = projected[:, q_cols:]
    kv_every = lax.all_gather(kv_part, "tp", axis=1, tiled=True)
    first_kv = tp_index * heads_here // group
    key_cols = lax.dynamic_slice_in_dim(kv_every, first_kv * HD, kv_here * HD, 1)
    value_cols = lax.dynamic_slice_in_dim(kv_every, KVH * HD + first_kv * HD, kv_here * HD, 1)
    kv_mine = jnp.concatenate([key_cols, value_cols], axis=1)
    block_starts = [ctx_index * ctx_rows + b * block_rows for b in range(n_ctx)]
    q_blocks = queries.reshape(n_ctx, block_rows, kv_here, sub_heads, HD).transpose(0, 2, 3, 1, 4)
    q_positions = [
        start_row + jnp.arange(block_rows, dtype=jnp.int32) for start_row in block_starts
    ]
    q_docs = [doc_index(pos, ends) for pos in q_positions]
    piece = gathered_copies(kv_mine, "ctx", 0)
    top_all = jnp.full((n_ctx, kv_here, sub_heads, block_rows), -1e30, jnp.float32)
    total_all = jnp.zeros((n_ctx, kv_here, sub_heads, block_rows), jnp.float32)
    acc_all = jnp.zeros((n_ctx, kv_here, sub_heads, block_rows, HD), jnp.float32)
    count = piece.shape[0]
    key_piece = piece[:, : kv_here * HD].reshape(count, kv_here, HD)
    value_piece = piece[:, kv_here * HD :].reshape(count, kv_here, HD)
    key_pos = jnp.arange(count, dtype=jnp.int32)
    key_doc = doc_index(key_pos, ends)
    new_top = []
    new_total = []
    new_acc = []
    for block in range(n_ctx):
        q_here = q_blocks[block]
        q_pos = q_positions[block]
        q_doc = q_docs[block]
        state = (top_all[block], total_all[block], acc_all[block])
        top_old, total_old, acc_old = state
        scores = (
            jnp.einsum("ghqd,kgd->ghqk", q_here, key_piece, preferred_element_type=jnp.float32)
            * scale
        )
        visible = (key_doc[None, :] == q_doc[:, None]) & (key_pos[None, :] <= q_pos[:, None])
        scores = jnp.where(visible[None, None], scores, jnp.float32(-1e30))
        top_new = jnp.maximum(top_old, jnp.max(scores, axis=3))
        expd = jnp.where(
            visible[None, None], jnp.exp(scores - top_new[..., None]), jnp.float32(0.0)
        )
        total_new = jnp.sum(expd, axis=3)
        acc_new = jnp.einsum(
            "ghqk,kgd->ghqd",
            expd.astype(jnp.bfloat16),
            value_piece,
            preferred_element_type=jnp.float32,
        )
        state = (top_new, total_new, acc_new)
        new_top.append(state[0])
        new_total.append(state[1])
        new_acc.append(state[2])
    total_all = jnp.stack(new_total)
    acc_all = jnp.stack(new_acc)
    heads_out = (acc_all / total_all[..., None]).astype(jnp.bfloat16)
    heads_out = heads_out.transpose(0, 3, 1, 2, 4).reshape(ctx_rows, q_cols)
    return lax.psum_scatter(
        jnp.dot(heads_out, out_weight, preferred_element_type=jnp.float32).astype(jnp.bfloat16),
        "tp",
        scatter_dimension=0,
        tiled=True,
    )


def solution(mesh):
    placed = (
        P(("dp", "ctx", "tp"), None),
        P(),
        P(None, "tp"),
        P(None, "tp"),
        P("tp", None),
        P("dp"),
    )
    return jax.shard_map(
        local, mesh=mesh, in_specs=placed, out_specs=P(("dp", "ctx", "tp"), None), check_vma=False
    )
```

profile of v0, /device:TPU:1, one launch (start us, length us, event | category | flops | bytes accessed | tf_op | source)
XLA Modules:
  0.0 425.1 jit_solution(6359207053137103046)
XLA Ops:
  8.2 2.5 fusion.30
  12.5 112.6 %all-gather.3.cloned.1.call-done = bf16[1024,8192]{1,0:T(8,128)(2,1)} async-done(((bf16[64,8192]{1,0:T(8,128)(2,1)}), bf16[1024,8192]{1,0:T(8,128)(2,1)}) %all-gather.3.cloned.1.call-update) | async-done | bytes 16777232 | tf_op jit(solution)/shard_map/all_gather | solution.py:84
  125.0 11.4 %fusion.73 = f32[1024,128]{0,1:T(8,128)S(1)} fusion(bf16[1024,8192]{1,0:T(8,128)(2,1)} %all-gather.3.cloned.1.call-done, bf16[8192,128]{1,0:T(8,128)(2,1)S(1)} %copy-done), kind=kOutput, calls=%fused_computation.116 | convolution fusion | flops 2147483648 | bytes 19398656 | tf_op jit(solution)/shard_map/dot_general | solution.py:89
  138.7 3.1 multiply_cosine_fusion
  141.7 6.3 %fusion.24 = (pred[256,4096]{1,0:T(8,128)(4,1)}, pred[256,4096]{1,0:T(8,128)(4,1)}, pred[256,4096]{1,0:T(8,128)(4,1)}, pred[256,4096]{1,0:T(8,128)(4,1)S(1)}) fusion(s32[256]{0:T(256)S(1)} %iota_add_fusion.4, s32[4096]{0:T(1024)S(1)} %convert_reduce_fusion, s32[256]{0:T(256)S(1)} %get-tuple-element.5, s32[256]{0:T(256)S(1)} %iota_add_fusion.3, ...), kind=kLoop, calls=%fused_computation.33 | loop fusion | flops 12582912 | bytes 4218880 | tf_op jit(solution)/shard_map/and | solution.py:128
  148.1 41.5 %all-gather.5.cloned.1.call-done = bf16[1024,2048]{0,1:T(8,128)(2,1)} async-done(((bf16[1024,128]{0,1:T(8,128)(2,1)}), bf16[1024,2048]{0,1:T(8,128)(2,1)}) %all-gather.5.cloned.1.call-update) | async-done | bytes 4194320 | tf_op jit(solution)/shard_map/all_gather | solution.py:95
  192.3 5.2 %all-to-all-start = ((bf16[4,1024,256]{2,1,0:T(8,128)(2,1)}), bf16[4,1024,256]{2,1,0:T(8,128)(2,1)}, u32[]{:S(2)}, u32[]{:S(2)}) async-start(bf16[4,1024,256]{2,1,0:T(8,128)(2,1)} %broadcast_in_dim.65), calls=%async_computation | async-start | bytes 4194304 | tf_op jit(solution)/shard_map/all_to_all | solution.py:15
  198.1 17.2 %fusion.72 = f32[1024,512]{0,1:T(8,128)S(1)} fusion(bf16[1024,8192]{1,0:T(8,128)(2,1)} %all-gather.3.cloned.1.call-done, bf16[8192,512]{1,0:T(8,128)(2,1)} %param.8), kind=kOutput, calls=%fused_computation.115 | convolution fusion | flops 8589934592 | bytes 27262976 | tf_op jit(solution)/shard_map/dot_general | solution.py:88
  218.7 3.2 copy.18
  221.9 2.4 subtract_convert_fusion
  226.0 5.0 %fusion = (f32[4,256]{1,0:T(4,128)S(1)}, f32[4,256,4096]{2,1,0:T(8,128)S(1)}) fusion(pred[256,4096]{1,0:T(8,128)(4,1)} %get-tuple-element.17, bf16[4096,256]{1,0:T(8,128)(2,1)} %bitcast.8, bf16[4,1,4,256,128]{4,3,2,1,0:T(8,128)(2,1)} %bitcast.85), kind=kOutput, calls=%fused_computation.9 | convolution fusion | flops 1086323712 | bytes 19140608 | tf_op jit(solution)/shard_map/ghqd,kgd->ghqk/dot_general | solution.py:125
  231.0 5.2 %fusion.4 = f32[4,256]{1,0:T(4,128)S(1)} fusion(f32[4,256,4096]{2,1,0:T(8,128)S(1)} %get-tuple-element.30, f32[4,256]{1,0:T(4,128)S(1)} %broadcast_maximum_fusion.3, pred[256,4096]{1,0:T(8,128)(4,1)S(1)} %copy-done.4), kind=kLoop, calls=%fused_computation.13 | loop fusion | flops 20970496 | bytes 17833984 | tf_op jit(solution)/shard_map/reduce_sum | solution.py:134
  236.3 6.3 %fusion.32 = f32[1,1,4,256,128]{4,3,2,1,0:T(8,128)S(1)} fusion(f32[4,256,4096]{2,1,0:T(8,128)S(1)} %get-tuple-element.30, f32[4,256]{1,0:T(4,128)S(1)} %broadcast_maximum_fusion.3, pred[256,4096]{1,0:T(8,128)(4,1)S(1)} %copy-done.5, bf16[4096,256]{1,0:T(8,128)(2,1)} %bitcast.8), kind=kOutput, calls=%fused_computation.46 | convolution fusion | flops 1094713344 | bytes 19402752 | tf_op jit(solution)/shard_map/ghqk,kgd->ghqd/dot_general | solution.py:135
  242.6 4.7 %fusion.1 = (f32[4,256]{1,0:T(4,128)S(1)}, f32[4,256,4096]{2,1,0:T(8,128)S(1)}) fusion(pred[256,4096]{1,0:T(8,128)(4,1)S(1)} %copy-done.3, bf16[4096,256]{1,0:T(8,128)(2,1)} %bitcast.8, bf16[4,1,4,256,128]{4,3,2,1,0:T(8,128)(2,1)S(1)} %bitcast.86), kind=kOutput, calls=%fused_computation.10 | convolution fusion | flops 1086323712 | bytes 19140608 | tf_op jit(solution)/shard_map/ghqd,kgd->ghqk/dot_general | solution.py:125
  247.3 5.3 %fusion.6 = f32[4,256]{1,0:T(4,128)S(1)} fusion(f32[4,256,4096]{2,1,0:T(8,128)S(1)} %get-tuple-element.28, f32[4,256]{1,0:T(4,128)S(1)} %broadcast_maximum_fusion.2, pred[256,4096]{1,0:T(8,128)(4,1)S(1)} %copy-done.3), kind=kLoop, calls=%fused_computation.15 | loop fusion | flops 20970496 | bytes 17833984 | tf_op jit(solution)/shard_map/reduce_sum | solution.py:134
  252.6 6.2 %fusion.35 = f32[1,1,4,256,128]{4,3,2,1,0:T(8,128)S(1)} fusion(f32[4,256,4096]{2,1,0:T(8,128)S(1)} %get-tuple-element.28, f32[4,256]{1,0:T(4,128)S(1)} %broadcast_maximum_fusion.2, pred[256,4096]{1,0:T(8,128)(4,1)S(1)} %copy-done.3, bf16[4096,256]{1,0:T(8,128)(2,1)} %bitcast.8), kind=kOutput, calls=%fused_computation.47 | convolution fusion | flops 1094713344 | bytes 19402752 | tf_op jit(solution)/shard_map/ghqk,kgd->ghqd/dot_general | solution.py:135
  258.8 4.7 %fusion.2 = (f32[4,256]{1,0:T(4,128)S(1)}, f32[4,256,4096]{2,1,0:T(8,128)S(1)}) fusion(pred[256,4096]{1,0:T(8,128)(4,1)S(1)} %copy-done.2, bf16[4096,256]{1,0:T(8,128)(2,1)} %bitcast.8, bf16[4,1,4,256,128]{4,3,2,1,0:T(8,128)(2,1)S(1)} %bitcast.87), kind=kOutput, calls=%fused_computation.11 | convolution fusion | flops 1086323712 | bytes 19140608 | tf_op jit(solution)/shard_map/ghqd,kgd->ghqk/dot_general | solution.py:125
  263.6 5.3 %fusion.8 = f32[4,256]{1,0:T(4,128)S(1)} fusion(f32[4,256,4096]{2,1,0:T(8,128)S(1)} %get-tuple-element.26, f32[4,256]{1,0:T(4,128)S(1)} %broadcast_maximum_fusion.1, pred[256,4096]{1,0:T(8,128)(4,1)S(1)} %copy-done.2), kind=kLoop, calls=%fused_computation.17 | loop fusion | flops 20970496 | bytes 17833984 | tf_op jit(solution)/shard_map/reduce_sum | solution.py:134
  268.9 6.1 %fusion.38 = f32[1,1,4,256,128]{4,3,2,1,0:T(8,128)S(1)} fusion(f32[4,256,4096]{2,1,0:T(8,128)S(1)} %get-tuple-element.26, f32[4,256]{1,0:T(4,128)S(1)} %broadcast_maximum_fusion.1, pred[256,4096]{1,0:T(8,128)(4,1)S(1)} %copy-done.2, bf16[4096,256]{1,0:T(8,128)(2,1)} %bitcast.8), kind=kOutput, calls=%fused_computation.48 | convolution fusion | flops 1094713344 | bytes 19402752 | tf_op jit(solution)/shard_map/ghqk,kgd->ghqd/dot_general | solution.py:135
  275.0 4.7 %fusion.3 = (f32[4,256]{1,0:T(4,128)S(1)}, f32[4,256,4096]{2,1,0:T(8,128)S(1)}) fusion(pred[256,4096]{1,0:T(8,128)(4,1)S(1)} %get-tuple-element.20, bf16[4096,256]{1,0:T(8,128)(2,1)} %bitcast.8, bf16[4,1,4,256,128]{4,3,2,1,0:T(8,128)(2,1)S(1)} %bitcast.88), kind=kOutput, calls=%fused_computation.12 | convolution fusion | flops 1086323712 | bytes 19140608 | tf_op jit(solution)/shard_map/ghqd,kgd->ghqk/dot_general | solution.py:125
  279.7 6.1 %fusion.41 = f32[1,1,4,256,128]{4,3,2,1,0:T(8,128)S(1)} fusion(f32[4,256,4096]{2,1,0:T(8,128)S(1)} %get-tuple-element.24, f32[4,256]{1,0:T(4,128)S(1)} %broadcast_maximum_fusion, pred[256,4096]{1,0:T(8,128)(4,1)S(1)} %get-tuple-element.20, bf16[4096,256]{1,0:T(8,128)(2,1)} %bitcast.8), kind=kOutput, calls=%fused_computation.49 | convolution fusion | flops 1094713344 | bytes 19402752 | tf_op jit(solution)/shard_map/ghqk,kgd->ghqd/dot_general | solution.py:135
  285.9 5.3 %fusion.10 = f32[4,256]{1,0:T(4,128)S(1)} fusion(f32[4,256,4096]{2,1,0:T(8,128)S(1)} %get-tuple-element.24, f32[4,256]{1,0:T(4,128)S(1)} %broadcast_maximum_fusion, pred[256,4096]{1,0:T(8,128)(4,1)S(1)} %get-tuple-element.20), kind=kLoop, calls=%fused_computation.19 | loop fusion | flops 20970496 | bytes 17833984 | tf_op jit(solution)/shard_map/reduce_sum | solution.py:134
  292.8 15.3 %convolution_convert_fusion = bf16[1024,8192]{1,0:T(8,128)(2,1)} fusion(bf16[512,8192]{1,0:T(8,128)(2,1)} %param.10, bf16[128,8,4,128]{3,2,1,0:T(4,128)(2,1)S(1)} %bitcast.89), kind=kOutput, calls=%fused_computation.8 | convolution fusion | flops 8598323200 | bytes 26214400 | tf_op jit(solution)/shard_map/dot_general | solution.py:150
  308.1 110.0 %reduce-scatter.2.cloned.1.call-done = bf16[64,8192]{1,0:T(8,128)(2,1)} async-done(((bf16[1024,8192]{1,0:T(8,128)(2,1)}), bf16[64,8192]{1,0:T(8,128)(2,1)}) %reduce-scatter.2.cloned.1.call-update) | async-done | bytes 1048592 | tf_op jit(solution)/shard_map/reduce_scatter | solution.py:149
  (50 shorter events, 15.4 us)
Async XLA Ops:
  6.5 118.5 %copy-start = (bf16[8192,128]{1,0:T(8,128)(2,1)S(1)}, bf16[8192,128]{1,0:T(8,128)(2,1)}, u32[]{:S(2)}) copy-start(bf16[8192,128]{1,0:T(8,128)(2,1)} %param.9) | copy-start | bytes 6291460
  6.5 118.5 %all-gather.3.cloned.1.call-start = ((), (), s32[]{:S(2)}) async-start(), calls=%async_computation.2 | async-start | bytes 17825792 | tf_op jit(solution)/shard_map/all_gather | solution.py:84
  10.8 178.8 %all-gather.5.cloned.1.call-start = ((), (), s32[]{:S(2)}) async-start(), calls=%async_computation.3 | async-start | bytes 4456448 | tf_op jit(solution)/shard_map/all_gather | solution.py:95
  192.3 33.7 %all-to-all-start = ((bf16[4,1024,256]{2,1,0:T(8,128)(2,1)}), bf16[4,1024,256]{2,1,0:T(8,128)(2,1)}, u32[]{:S(2)}, u32[]{:S(2)}) async-start(bf16[4,1024,256]{2,1,0:T(8,128)(2,1)} %broadcast_in_dim.65), calls=%async_computation | async-start | bytes 4194304 | tf_op jit(solution)/shard_map/all_to_all | solution.py:15
  197.5 220.6 %reduce-scatter.2.cloned.1.call-start = ((), (), s32[]{:S(2)}) async-start(), calls=%async_computation.4 | async-start | bytes 17825792 | tf_op jit(solution)/shard_map/reduce_scatter | solution.py:149
  224.3 6.7 %copy-start.4 = (pred[256,4096]{1,0:T(8,128)(4,1)S(1)}, pred[256,4096]{1,0:T(8,128)(4,1)}, u32[]{:S(2)}) copy-start(pred[256,4096]{1,0:T(8,128)(4,1)} %get-tuple-element.17) | copy-start | bytes 3145732
  226.0 10.3 %copy-start.5 = (pred[256,4096]{1,0:T(8,128)(4,1)S(1)}, pred[256,4096]{1,0:T(8,128)(4,1)}, u32[]{:S(2)}) copy-start(pred[256,4096]{1,0:T(8,128)(4,1)} %get-tuple-element.17) | copy-start | bytes 3145732
  236.3 6.3 %copy-start.3 = (pred[256,4096]{1,0:T(8,128)(4,1)S(1)}, pred[256,4096]{1,0:T(8,128)(4,1)}, u32[]{:S(2)}) copy-start(pred[256,4096]{1,0:T(8,128)(4,1)} %get-tuple-element.18) | copy-start | bytes 3145732
  236.3 6.3 %copy-start.6 = (bf16[4,256,1,4,128]{4,1,3,2,0:T(8,128)(2,1)S(1)}, bf16[4,256,1,4,128]{4,1,3,2,0:T(8,128)(2,1)}, u32[]{:S(2)}) copy-start(bf16[4,256,1,4,128]{4,1,3,2,0:T(8,128)(2,1)} %copy.26) | copy-start | bytes 3145732
  252.6 6.2 %copy-start.2 = (pred[256,4096]{1,0:T(8,128)(4,1)S(1)}, pred[256,4096]{1,0:T(8,128)(4,1)}, u32[]{:S(2)}) copy-start(pred[256,4096]{1,0:T(8,128)(4,1)} %get-tuple-element.19) | copy-start | bytes 3145732
  292.8 125.3 %copy-start.1 = (bf16[8192,128]{1,0:T(8,128)(2,1)S(1)}, bf16[8192,128]{1,0:T(8,128)(2,1)}, u32[]{:S(2)}) copy-start(bf16[8192,128]{1,0:T(8,128)(2,1)} %param.9) | copy-start | bytes 6291460
Sparse Core Ops, SparseCore 0:
  10.9 114.0 all-gather.2
  138.5 50.9 all-gather.4
  308.2 109.8 reduce-scatter.1
where the time goes:
time: 432 us; the launch traced here: 425 us
  waiting for transfers between devices  264 us (61%)
  matrix products  87.8 us (20%)
  other arithmetic  42.2 us (10%)
  between operations  14 us (3%)
  local copies, waits for them, and re-layouts  11.2 us (3%)
  starting transfers between devices  5.8 us (1%)
    all_gather x1, waiting for transfers between devices, local(): piece = lax.all_gather(normed, 'tp', axis=0, tiled=True)  113 us
    reduce_scatter x1, waiting for transfers between devices, local(): lax.psum_scatter(jnp.dot(heads_out, out_weight, preferred_element_type=jn...  110 us
    all_gather x1, waiting for transfers between devices, local(): kv_every = lax.all_gather(kv_part, 'tp', axis=1, tiled=True)  41.5 us
    dot_general x4, matrix products, local(): jnp.einsum('ghqk,kgd->ghqd', expd.astype(jnp.bfloat16), value_piece, pref...  24.7 us
    reduce_sum x4, other arithmetic, local(): total_new = jnp.sum(expd, axis=3)  21.1 us
    dot_general x4, matrix products, local(): jnp.einsum('ghqd,kgd->ghqk', q_here, key_piece, preferred_element_type=jn...  19.2 us
    dot_general x1, matrix products, local(): q_raw = jnp.dot(piece, q_weight, preferred_element_type=jnp.float32)  17.2 us
    dot_general x1, matrix products, local(): jnp.dot(heads_out, out_weight, preferred_element_type=jnp.float32)  15.3 us
  transfers between devices with their start and end apart: 4, of which 3 were waited for; matrix products, arithmetic and copies ran while one was open for 9% of the time, Pallas kernels for 0%

commit v1 on v0

v1 whole, which is shorter than its diff:
```python
import functools
import math

import jax
import jax.numpy as jnp
from jax import lax
from jax.experimental import pallas as pl
from jax.experimental.pallas import tpu as pltpu
from jax.sharding import PartitionSpec as P

QH = 64
KVH = 8
HD = 128


def from_everyone(shard, axis):
    length = lax.axis_size(axis)
    return lax.all_to_all(
        jnp.broadcast_to(shard[None], (length, *shard.shape)), axis, 0, 0, tiled=True
    )


def laid_out(blocks, dim):
    blocks = jnp.moveaxis(blocks, 0, dim)
    shape = blocks.shape
    return blocks.reshape(*shape[:dim], shape[dim] * shape[dim + 1], *shape[dim + 2 :])


def gathered_copies(shard, axis, dim):
    blocks = from_everyone(shard, axis)
    return laid_out(blocks, dim)


def doc_start(positions, lengths, ends):
    return jnp.sum(jnp.where(positions[:, None] >= ends[None, :], lengths[None, :], 0), axis=1)


def rope_freqs(half):
    base = jnp.power(jnp.float32(500000.0), -(jnp.arange(half, dtype=jnp.float32) * 2.0) / HD)
    wavelen = 2.0 * math.pi / base
    smooth = (8192.0 / wavelen - 1.0) / 3.0
    middle = (1.0 - smooth) * base / 8.0 + smooth * base
    return jnp.where(wavelen < 2048.0, base, jnp.where(wavelen > 8192.0, base / 8.0, middle))


def rotate(values, within):
    rows = values.shape[0]
    blocks = values.reshape(rows, values.shape[1] // HD, HD)
    half = HD // 2
    freqs = rope_freqs(half)
    angles = within.astype(jnp.float32)[:, None] * freqs[None, :]
    cosine = jnp.cos(angles)[:, None, :]
    sine = jnp.sin(angles)[:, None, :]
    first = blocks[:, :, :half]
    second = blocks[:, :, half:]
    turned = jnp.concatenate(
        [first * cosine - second * sine, second * cosine + first * sine], axis=2
    )
    return turned.reshape(rows, values.shape[1])


def attn_kernel(heads, bq, bk, docs, info_ref, q_ref, k_ref, v_ref, o_ref, acc_ref):
    first = info_ref[0] + pl.program_id(0) * bq
    last = first + bq - 1
    rows = first + lax.broadcasted_iota(jnp.int32, (1, bq), 1)
    low = jnp.zeros((1, bq), jnp.int32)
    low_first = jnp.int32(0)
    for d in range(docs):
        end = info_ref[1 + d]
        low = jnp.where(rows >= end, jnp.maximum(low, end), low)
        low_first = jnp.where(first >= end, jnp.maximum(low_first, end), low_first)
    factor = HD ** (-0.5) * math.log2(math.e)
    acc_ref[...] = jnp.zeros_like(acc_ref)

    def step(i, state):
        at = pl.multiple_of(i * bk, bk)
        key = k_ref[pl.ds(at, bk), :]
        value = v_ref[pl.ds(at, bk), :]
        index = at + lax.broadcasted_iota(jnp.int32, (bk, 1), 0)
        visible = (index >= low) & (index <= rows)
        out = []
        for h in range(heads):
            top, total = state[h]
            scores = lax.dot_general(
                key, q_ref[:, h * HD : (h + 1) * HD], (((1,), (1,)), ((), ())), preferred_element_type=jnp.float32
            )
            scores = jnp.where(visible, scores * factor, jnp.float32(-1e30))
            new = jnp.maximum(top, jnp.max(scores, axis=0, keepdims=True))
            keep = jnp.exp2(top - new)
            expd = jnp.exp2(scores - new)
            total = total * keep + jnp.sum(expd, axis=0, keepdims=True)
            acc_ref[h] = acc_ref[h] * keep + lax.dot_general(
                value, expd.astype(jnp.bfloat16), (((0,), (0,)), ((), ())), preferred_element_type=jnp.float32
            )
            out.append((new, total))
        return tuple(out)

    start = tuple((jnp.full((1, bq), -1e30, jnp.float32), jnp.zeros((1, bq), jnp.float32)) for _ in range(heads))
    state = lax.fori_loop(low_first // bk, last // bk + 1, step, start)
    for h in range(heads):
        o_ref[:, h * HD : (h + 1) * HD] = (acc_ref[h] / state[h][1]).T.astype(o_ref.dtype)

def attention(info, q, k, v, heads, bq=256, bk=256, docs=8):
    rows = q.shape[0]
    return pl.pallas_call(
        functools.partial(attn_kernel, heads, bq, bk, docs),
        grid_spec=pltpu.PrefetchScalarGridSpec(
            num_scalar_prefetch=1,
            grid=(rows // bq,),
            in_specs=[
                pl.BlockSpec((bq, heads * HD), lambda i, s: (i, 0)),
                pl.BlockSpec((k.shape[0], HD), lambda i, s: (0, 0)),
                pl.BlockSpec((v.shape[0], HD), lambda i, s: (0, 0)),
            ],
            out_specs=pl.BlockSpec((bq, heads * HD), lambda i, s: (i, 0)),
            scratch_shapes=[pltpu.VMEM((heads, HD, bq), jnp.float32)],
        ),
        out_shape=jax.ShapeDtypeStruct((rows, heads * HD), jnp.bfloat16),
        compiler_params=pltpu.CompilerParams(vmem_limit_bytes=40 * 2**20),
        name="attention",
    )(info, q, k, v)


def local(hidden_in, norm_gain, q_weight, kv_weight, out_weight, doc_lengths):
    tok_rows = hidden_in.shape[0]
    n_tp = lax.axis_size("tp")
    ctx_rows = tok_rows * n_tp
    q_cols = q_weight.shape[1]
    heads_here = q_cols // HD
    kv_cols = kv_weight.shape[1]
    tp_index = lax.axis_index("tp")
    ctx_index = lax.axis_index("ctx")
    x = hidden_in.astype(jnp.float32)
    normed = (
        x * lax.rsqrt(jnp.mean(x * x, axis=1, keepdims=True) + 1e-05) * norm_gain[None, :]
    ).astype(jnp.bfloat16)
    ends = jnp.cumsum(doc_lengths)
    is_key = tp_index * kv_cols < KVH * HD
    piece = lax.all_gather(normed, "tp", axis=0, tiled=True)
    count = piece.shape[0]
    positions = ctx_index * ctx_rows + jnp.arange(count, dtype=jnp.int32)
    within = positions - doc_start(positions, doc_lengths, ends)
    q_raw = jnp.dot(piece, q_weight, preferred_element_type=jnp.float32)
    kv_raw = jnp.dot(piece, kv_weight, preferred_element_type=jnp.float32)
    q_done = rotate(q_raw, within).astype(jnp.bfloat16)
    kv_done = jnp.where(is_key, rotate(kv_raw, within), kv_raw).astype(jnp.bfloat16)
    projected = jnp.concatenate([q_done, kv_done], axis=1)
    queries = projected[:, :q_cols]
    kv_part = projected[:, q_cols:]
    half = lax.axis_size("tp") // 2
    same = [(i, 2 * i) for i in range(half)] + [(half + i, 2 * i + 1) for i in range(half)]
    other = [(i, 2 * i + 1) for i in range(half)] + [(half + i, 2 * i) for i in range(half)]
    one = lax.ppermute(kv_part, "tp", same)
    two = lax.ppermute(kv_part, "tp", other)
    even = tp_index % 2 == 0
    kv_mine = jnp.concatenate([jnp.where(even, one, two), jnp.where(even, two, one)], axis=1)
    piece = gathered_copies(kv_mine, "ctx", 0)
    info = jnp.concatenate([(ctx_index * ctx_rows)[None], ends]).astype(jnp.int32)
    heads_out = attention(info, queries, piece[:, :HD], piece[:, HD:], heads_here, docs=doc_lengths.shape[0])
    return lax.psum_scatter(
        jnp.dot(heads_out, out_weight, preferred_element_type=jnp.float32).astype(jnp.bfloat16),
        "tp",
        scatter_dimension=0,
        tiled=True,
    )


def solution(mesh):
    placed = (
        P(("dp", "ctx", "tp"), None),
        P(),
        P(None, "tp"),
        P(None, "tp"),
        P("tp", None),
        P("dp"),
    )
    return jax.shard_map(
        local, mesh=mesh, in_specs=placed, out_specs=P(("dp", "ctx", "tp"), None), check_vma=False
    )
```

time: 432 us -> 356 us (0.82)
  matrix products: 87.8 us -> 42.4 us
  other arithmetic: 42.2 us -> 13 us
  Pallas kernels: 0 us -> 15.8 us
  waiting for transfers between devices: 264 us -> 251 us
    dot_general x8 -> x0, matrix products: 43.9 us -> none  [the longest x4 24.7 us: local(): jnp.einsum('ghqk,kgd->ghqd', expd.astype(jnp.bfloat16), value_piece, pref...]
    all_gather x1 -> x0, waiting for transfers between devices: 41.5 us -> none  [local(): kv_every = lax.all_gather(kv_part, 'tp', axis=1, tiled=True)]
    reduce_scatter x1, waiting for transfers between devices: 110 us -> 134 us  [local(): lax.psum_scatter(jnp.dot(heads_out, out_weight, preferred_element_type=jn...]
    reduce_sum x6 -> x0, other arithmetic: 21.3 us -> none  [the longest x4 21.1 us: local(): total_new = jnp.sum(expd, axis=3)]
    pallas_call x0 -> x1, Pallas kernels: none -> 15.8 us  [attention(): pl.pallas_call(functools.partial(attn_kernel, heads, bq, bk, docs), grid_...]
    and x1 -> x0, other arithmetic: 6.31 us -> none  [local(): (key_doc[None, :] == q_doc[:, None]) & (key_pos[None, :] <= q_pos[:, None])]
  transfers between devices with their start and end apart: 4 -> 5, of which waited for: 3 -> 3; matrix products, arithmetic and copies ran while one was open for 9% -> 8% of each run, Pallas kernels for 0% -> 0%
where the time goes in v1:
time: 356 us; the launch traced here: 353 us
  waiting for transfers between devices  251 us (71%)
  matrix products  42.4 us (12%)
  Pallas kernels  15.8 us (4%)
  between operations  13.6 us (4%)
  other arithmetic  13 us (4%)
  local copies, waits for them, and re-layouts  8.8 us (2%)
  starting transfers between devices  8.05 us (2%)
    reduce_scatter x1, waiting for transfers between devices, local(): lax.psum_scatter(jnp.dot(heads_out, out_weight, preferred_element_type=jn...  134 us
    all_gather x1, waiting for transfers between devices, local(): piece = lax.all_gather(normed, 'tp', axis=0, tiled=True)  114 us
    dot_general x1, matrix products, local(): q_raw = jnp.dot(piece, q_weight, preferred_element_type=jnp.float32)  15.9 us
    pallas_call x1, Pallas kernels, attention(): pl.pallas_call(functools.partial(attn_kernel, heads, bq, bk, docs), grid_...  15.8 us
    dot_general x1, matrix products, local(): jnp.dot(heads_out, out_weight, preferred_element_type=jnp.float32)  15.1 us
    dot_general x1, matrix products, local(): kv_raw = jnp.dot(piece, kv_weight, preferred_element_type=jnp.float32)  11.4 us
  transfers between devices with their start and end apart: 5, of which 3 were waited for; matrix products, arithmetic and copies ran while one was open for 8% of the time, Pallas kernels for 0%

profile of v1, /device:TPU:1, one launch (start us, length us, event | category | flops | bytes accessed | tf_op | source)
XLA Modules:
  0.0 352.9 jit_solution(13213593132613575509)
XLA Ops:
  6.5 1.7 fusion
  8.2 2.5 fusion.2
  10.8 0.2 reduce-window.8
  11.1 113.9 %all-gather.2.cloned.1.call-done = bf16[1024,8192]{1,0:T(8,128)(2,1)} async-done(((bf16[64,8192]{1,0:T(8,128)(2,1)}), bf16[1024,8192]{1,0:T(8,128)(2,1)}) %all-gather.2.cloned.1.call-update) | async-done | bytes 16777232 | tf_op jit(solution)/shard_map/all_gather | solution.py:139
  125.0 11.4 %fusion.14 = f32[1024,128]{0,1:T(8,128)S(1)} fusion(bf16[1024,8192]{1,0:T(8,128)(2,1)} %all-gather.2.cloned.1.call-done, bf16[8192,128]{1,0:T(8,128)(2,1)S(1)} %copy-done), kind=kOutput, calls=%fused_computation.36 | convolution fusion | flops 2147483648 | bytes 19398656 | tf_op jit(solution)/shard_map/dot_general | solution.py:144
  136.5 1.2 fusion.9
  137.7 1.3 collective-permute-start.1
  139.0 0.7 collective-permute-start
  139.7 2.9 multiply_cosine_fusion
  142.6 3.6 %collective-permute-done.1 = bf16[1024,128]{0,1:T(8,128)(2,1)S(1)} collective-permute-done((bf16[1024,128]{0,1:T(8,128)(2,1)S(1)}, bf16[1024,128]{0,1:T(8,128)(2,1)S(1)}, u32[]{:S(2)}, u32[]{:S(2)}) %collective-permute-start.1) | collective-permute-done | bytes 262176 | tf_op jit(solution)/shard_map/ppermute | solution.py:154
  146.4 0.2 copy.12
  146.6 1.4 broadcast_in_dim.19
  148.0 6.1 %all-to-all-start = ((bf16[4,1024,256]{2,1,0:T(8,128)(2,1)}), bf16[4,1024,256]{2,1,0:T(8,128)(2,1)}, u32[]{:S(2)}, u32[]{:S(2)}) async-start(bf16[4,1024,256]{2,1,0:T(8,128)(2,1)} %broadcast_in_dim.19), calls=%async_computation | async-start | bytes 4194304 | tf_op jit(solution)/shard_map/all_to_all | solution.py:18
  154.1 15.9 %fusion.13 = f32[1024,512]{0,1:T(8,128)} fusion(bf16[1024,8192]{1,0:T(8,128)(2,1)} %all-gather.2.cloned.1.call-done, bf16[8192,512]{1,0:T(8,128)(2,1)} %param.8), kind=kOutput, calls=%fused_computation.35 | convolution fusion | flops 8589934592 | bytes 27262976 | tf_op jit(solution)/shard_map/dot_general | solution.py:143
  170.0 1.7 fusion.12
  171.8 1.8 copy.14
  173.6 1.8 copy.13
  175.3 2.8 subtract_convert_fusion
  178.1 1.4 pad_maximum_fusion
  179.5 0.2 copy.17
  179.7 1.7 fusion.11
  181.4 15.8 %attention.1 = bf16[1024,512]{1,0:T(8,128)(2,1)S(1)} custom-call(s32[9]{0:T(128)S(1)} %pad_add_fusion.info_ref, bf16[1024,512]{1,0:T(8,128)(2,1)S(1)} %bitcast.22, bf16[4096,128]{1,0:T(8,128)(2,1)S(1)} %get-tuple-element.8.k_ref, bf16[4096,128]{1,0:T(8,128)(2,1)S(1)} %get-tuple-element.7.v_ref), custom_call_target="tpu_custom_call" | custom-call | tf_op jit(solution)/shard_map/attention/pallas_call | solution.py:105
  197.2 15.1 %convolution_convert_fusion = bf16[1024,8192]{1,0:T(8,128)(2,1)} fusion(bf16[1024,512]{1,0:T(8,128)(2,1)S(1)} %attention.1, bf16[512,8192]{1,0:T(8,128)(2,1)} %param.10), kind=kOutput, calls=%fused_computation | convolution fusion | flops 8598323200 | bytes 26214400 | tf_op jit(solution)/shard_map/dot_general | solution.py:161
  212.3 133.8 %reduce-scatter.2.cloned.1.call-done = bf16[64,8192]{1,0:T(8,128)(2,1)} async-done(((bf16[1024,8192]{1,0:T(8,128)(2,1)}), bf16[64,8192]{1,0:T(8,128)(2,1)}) %reduce-scatter.2.cloned.1.call-update) | async-done | bytes 1048592 | tf_op jit(solution)/shard_map/reduce_scatter | solution.py:160
  (23 shorter events, 0.4 us)
Async XLA Ops:
  6.5 118.5 %copy-start = (bf16[8192,128]{1,0:T(8,128)(2,1)S(1)}, bf16[8192,128]{1,0:T(8,128)(2,1)}, u32[]{:S(2)}) copy-start(bf16[8192,128]{1,0:T(8,128)(2,1)} %param.9) | copy-start | bytes 6291460
  6.5 4.3 %copy-start.3 = (s32[8]{0:T(128)S(1)}, s32[8]{0:T(128)}, u32[]{:S(2)}) copy-start(s32[8]{0:T(128)} %param.11) | copy-start | bytes 100
  6.5 118.5 %all-gather.2.cloned.1.call-start = ((), (), s32[]{:S(2)}) async-start(), calls=%async_computation.2 | async-start | bytes 17825792 | tf_op jit(solution)/shard_map/all_gather | solution.py:139
  137.7 8.6 %collective-permute-start.1 = (bf16[1024,128]{0,1:T(8,128)(2,1)S(1)}, bf16[1024,128]{0,1:T(8,128)(2,1)S(1)}, u32[]{:S(2)}, u32[]{:S(2)}) collective-permute-start(bf16[1024,128]{0,1:T(8,128)(2,1)S(1)} %fusion.4), channel_id=1, source_target_pairs={{0,2},{2,6},{4,10},{6,14},{8,18},{10,22},{12,26},{14,30},{16,0},{1... | collective-permute-start | bytes 786440 | tf_op jit(solution)/shard_map/ppermute | solution.py:154
  139.0 7.3 %collective-permute-start = (bf16[1024,128]{0,1:T(8,128)(2,1)S(1)}, bf16[1024,128]{0,1:T(8,128)(2,1)S(1)}, u32[]{:S(2)}, u32[]{:S(2)}) collective-permute-start(bf16[1024,128]{0,1:T(8,128)(2,1)S(1)} %fusion.4), channel_id=1, source_target_pairs={{0,0},{2,4},{4,8},{6,12},{8,16},{10,20},{12,24},{14,28},{16,2},{18... | collective-permute-start | bytes 786440 | tf_op jit(solution)/shard_map/ppermute | solution.py:153
  148.0 31.7 %all-to-all-start = ((bf16[4,1024,256]{2,1,0:T(8,128)(2,1)}), bf16[4,1024,256]{2,1,0:T(8,128)(2,1)}, u32[]{:S(2)}, u32[]{:S(2)}) async-start(bf16[4,1024,256]{2,1,0:T(8,128)(2,1)} %broadcast_in_dim.19), calls=%async_computation | async-start | bytes 4194304 | tf_op jit(solution)/shard_map/all_to_all | solution.py:18
  154.1 192.0 %reduce-scatter.2.cloned.1.call-start = ((), (), s32[]{:S(2)}) async-start(), calls=%async_computation.3 | async-start | bytes 17825792 | tf_op jit(solution)/shard_map/reduce_scatter | solution.py:160
  173.6 1.8 copy-start.2
  212.3 133.8 %copy-start.1 = (bf16[8192,128]{1,0:T(8,128)(2,1)S(1)}, bf16[8192,128]{1,0:T(8,128)(2,1)}, u32[]{:S(2)}) copy-start(bf16[8192,128]{1,0:T(8,128)(2,1)} %param.9) | copy-start | bytes 6291460
Sparse Core Ops, SparseCore 0:
  10.9 114.0 all-gather.1
  212.4 133.6 reduce-scatter.1
